TPU v7x, 128 devices: a whole 4x4x4 slice. The times are simulated.
128 devices in a mesh: table: 8 (over y, core), ray: 16 (over x, z).
Axes of the slice: x: 4, y: 4, z: 4, core: 2. Of those that a mesh axis runs over, the one named last changes fastest.
Arguments:
- table: float32 [2, 8192, 4, 512], P(None, ('table', 'ray')), may hold values from -6 to 6
- moment1: float32 [2, 8192, 4, 512], P(None, ('table', 'ray')), may hold values from -2 to 2
- moment2: float32 [2, 8192, 4, 512], P(None, ('table', 'ray')), may hold values from 0.01 to 1
- block_ids: int32 [8, 2, 128, 4], replicated, may hold values from 0 to 63, as said below
- sample_slot: int32 [2, 65536], P(None, ('table', 'ray')), may hold values from 0 to 511, as said below
- corners: int32 [2, 8, 65536], P(None, None, ('table', 'ray')), may hold values from 0 to 511
- fractions: float32 [2, 3, 65536], P(None, None, ('table', 'ray')), may hold values from 0 to 1
- feat_cot: float32 [2, 4, 65536], P(None, None, ('table', 'ray')), may hold values from -24 to 24
- weight_in: float32 [64, 8], replicated, may hold values from -2 to 2
- weight_out: float32 [16, 64], replicated, may hold values from -0.75 to 0.75
Outputs:
- table_new: float32 [2, 8192, 4, 512], P(None, ('table', 'ray'))
- moment1_new: float32 [2, 8192, 4, 512], P(None, ('table', 'ray'))
- moment2_new: float32 [2, 8192, 4, 512], P(None, ('table', 'ray'))
- mlp_out: float32 [16, 65536], P(None, ('table', 'ray'))
Inputs may be any that keep to these rules, and one draw needn't show every extreme that they name: `block_ids`: for every group, level and owner the 4 listed blocks are distinct local block numbers of that owner. `sample_slot`: each device's 512 samples of a level come in 16 runs of 512 // 16 in order; the samples of run i read only blocks of owners o with o % 16 == i.
All inputs are finite; a program needn't handle non-finite values.
Results may differ from a plain program's by a relative error of at most 0.000075.
Values sent between devices are 32-bit elements; how exact they have to be, the bound alone decides.
No kernel may reach another device: no remote copies, remote signals or barrier semaphores. Data moves between devices by JAX's collectives and lax.ppermute only.
A program may use at most 64 MiB of HBM per device.

v0:
```python
import jax
import jax.numpy as jnp
from jax import lax
from jax.sharding import PartitionSpec as P

beta_one = 0.9
beta_two = 0.99
learn_rate = 0.01
adam_eps = 1e-15


def hat_weights(fractions):
    columns = []
    for corner in range(8):
        weight = jnp.ones_like(fractions[:, 0, :])
        for dimension in range(3):
            if corner >> dimension & 1:
                weight = weight * fractions[:, dimension, :]
            else:
                weight = weight * (1.0 - fractions[:, dimension, :])
        columns.append(weight)
    return jnp.stack(columns, axis=1)


def corner_spread(weights, corners, block_rows):
    entry = jnp.arange(block_rows, dtype=jnp.int32)
    total = jnp.zeros(weights[:, 0].shape + (block_rows,), jnp.float32)
    for corner in range(8):
        hit = corners[:, corner, :, :, None] == entry
        total = total + jnp.where(hit, weights[:, corner, :, :, None], 0.0)
    return total


def candidate_onehot(slots, ray_size, slot_count, candidates):
    local_slot = slots // slot_count // ray_size * slot_count + slots % slot_count
    return (local_slot[..., None] == jnp.arange(candidates, dtype=jnp.int32)).astype(jnp.float32)


def block_partials(onehot, cot, spread):
    levels, runs, run_len, candidates = onehot.shape
    cot_rows = jnp.transpose(cot, (0, 2, 3, 1))
    scaled = onehot[:, :, :, :, None] * cot_rows[:, :, :, None, :]
    scaled = scaled.reshape(levels, runs, run_len, candidates * 4)
    return jnp.einsum("lrjc,lrje->lrce", scaled, spread, precision=lax.Precision.HIGHEST)


def on_device(
    table,
    moment1,
    moment2,
    block_ids,
    sample_slot,
    corners,
    fractions,
    feat_cot,
    weight_in,
    weight_out,
):
    table_size = lax.axis_size("table")
    ray_size = lax.axis_size("ray")
    levels, blocks_dev, features, block_rows = table.shape
    slot_count = block_ids.shape[3]
    samples = sample_slot.shape[1]
    candidates = table_size * slot_count
    run_len = samples // ray_size
    owner_here = lax.axis_index("table") * ray_size + lax.axis_index("ray")
    weights = hat_weights(fractions)
    spread = corner_spread(
        weights.reshape(levels, 8, ray_size, run_len),
        corners.reshape(levels, 8, ray_size, run_len),
        block_rows,
    )
    onehot = candidate_onehot(
        sample_slot.reshape(levels, ray_size, run_len), ray_size, slot_count, candidates
    )
    partial_value = block_partials(onehot, feat_cot.reshape(levels, 4, ray_size, run_len), spread)
    partial_value = partial_value.reshape(levels, ray_size, table_size, slot_count, 4, block_rows)
    partial_value = jnp.transpose(partial_value, (0, 2, 1, 3, 4, 5))
    routed = lax.all_to_all(partial_value, "table", split_axis=1, concat_axis=1, tiled=True)
    summed = lax.psum_scatter(routed, "ray", scatter_dimension=2, tiled=True)
    received = summed.reshape(levels, table_size * slot_count, 4 * block_rows)
    own_ids = lax.dynamic_index_in_dim(block_ids, owner_here, axis=2, keepdims=False)
    requests = jnp.transpose(own_ids, (1, 0, 2)).reshape(levels, table_size * slot_count)
    block_range = jnp.arange(blocks_dev, dtype=jnp.int32)
    selector = (requests[:, None, :] == block_range[None, :, None]).astype(jnp.float32)
    gradient = jnp.einsum("lbk,lkf->lbf", selector, received, precision=lax.Precision.HIGHEST)
    gradient = gradient.reshape(table.shape)
    first_new = beta_one * moment1 + (1.0 - beta_one) * gradient
    second_new = beta_two * moment2 + (1.0 - beta_two) * gradient * gradient
    table_new = table - learn_rate * first_new / (jnp.sqrt(second_new) + adam_eps)
    flat_table = table_new.reshape(levels, blocks_dev, 4 * block_rows)
    picked = jnp.take_along_axis(flat_table, requests[:, :, None], axis=1)
    picked = picked.reshape(levels, table_size, 1, slot_count, 4, block_rows)
    returned = lax.all_to_all(picked, "table", split_axis=1, concat_axis=1, tiled=True)
    fetched = lax.all_gather(returned, "ray", axis=2, tiled=True)
    run_tables = jnp.transpose(fetched, (0, 2, 1, 3, 4, 5)).reshape(
        levels, ray_size, candidates * 4, block_rows
    )
    looked = jnp.einsum("lrje,lrce->lrjc", spread, run_tables, precision=lax.Precision.HIGHEST)
    looked = looked.reshape(levels, ray_size, run_len, candidates, 4)
    values = jnp.sum(onehot[:, :, :, :, None] * looked, axis=3)
    encoded = jnp.transpose(values, (0, 3, 1, 2)).reshape(4 * levels, samples)
    hidden = jax.nn.relu(jnp.dot(weight_in, encoded, precision=lax.Precision.HIGHEST))
    mlp_out = jnp.dot(weight_out, hidden, precision=lax.Precision.HIGHEST)
    return (table_new, first_new, second_new, mlp_out)


def solution(mesh):
    in_specs = (
        P(None, ("table", "ray"), None, None),
        P(None, ("table", "ray"), None, None),
        P(None, ("table", "ray"), None, None),
        P(),
        P(None, ("table", "ray")),
        P(None, None, ("table", "ray")),
        P(None, None, ("table", "ray")),
        P(None, None, ("table", "ray")),
        P(),
        P(),
    )
    out_specs = (
        P(None, ("table", "ray"), None, None),
        P(None, ("table", "ray"), None, None),
        P(None, ("table", "ray"), None, None),
        P(None, ("table", "ray")),
    )
    return jax.shard_map(
        on_device, mesh=mesh, in_specs=in_specs, out_specs=out_specs, check_vma=False
    )
```

profile of v0, /device:TPU:1, one launch (start us, length us, event | category | flops | bytes accessed | tf_op | source)
XLA Modules:
  0.0 376.9 jit_solution(16789116876656948793)
XLA Ops:
  7.2 0.7 fusion.14
  8.0 0.7 fusion.16
  8.8 0.8 reshape.206
  10.1 0.8 reshape.207
  10.9 0.8 reshape.208
  12.1 11.2 %fusion = f32[2,16,128,512]{3,2,1,0:T(8,128)} fusion(f32[2,16,32,128]{2,1,3,0:T(8,128)S(1)} %bitcast.64, f32[2,16,32]{2,1,0:T(8,128)S(1)} %broadcast_in_dim.107, s32[2,16,32]{2,1,0:T(8,128)S(1)} %get-tuple-element.8, f32[2,16,32]{2,1,0:T(8,128)S(1)} %broadcast_in_dim.105, s32[2,16,32]{2,1,0:T(8,128)S(1)} %get-tuple-element.9, ...), kind=kOutput, calls=%fused_computation.2 | convolution fusion | flops 817364992 | bytes 8978432 | tf_op jit(solution)/shard_map/lrjc,lrje->lrce/dot_general | solution.py:44
  23.4 9.8 %reshape.209 = f32[2,16,8,4,4,512]{5,4,3,2,1,0:T(4,128)} reshape(f32[2,16,128,512]{3,2,1,0:T(8,128)} %fusion) | data formatting | bytes 16777216 | tf_op jit(solution)/shard_map/reshape | solution.py:77
  33.1 10.3 %copy.52 = f32[2,16,8,4,4,512]{5,4,3,1,0,2:T(4,128)} copy(f32[2,16,8,4,4,512]{5,4,3,2,1,0:T(4,128)} %reshape.209) | data formatting | bytes 16777216 | tf_op jit(solution)/shard_map/reshape | solution.py:77
  43.5 99.5 %all_to_all.10 = f32[2,8,16,4,4,512]{5,4,3,2,0,1:T(4,128)S(1)} all-to-all(f32[2,8,16,4,4,512]{5,4,3,2,0,1:T(4,128)} %bitcast.61), channel_id=1, replica_groups=mesh['table'=8,'ray'=16] {'table'}, dimensions={1} | all-to-all | bytes 16777216 | tf_op jit(solution)/shard_map/all_to_all | solution.py:79
  143.0 10.9 %copy.41 = f32[2,8,16,4,4,512]{5,1,4,3,0,2:T(8,128)} copy(f32[2,8,16,4,4,512]{5,4,3,2,0,1:T(4,128)S(1)} %all_to_all.10) | data formatting | bytes 16777216 | tf_op jit(solution)/shard_map/all_to_all | solution.py:79
  154.9 85.0 %reduce-scatter.4.cloned.1.call-done = f32[2,8,1,4,4,512]{5,1,4,3,0,2:T(8,128)} async-done(((f32[2,8,16,4,4,512]{5,1,4,3,0,2:T(8,128)}), f32[2,8,1,4,4,512]{5,1,4,3,0,2:T(8,128)}) %reduce-scatter.4.cloned.1.call-update) | async-done | bytes 524304
  240.0 1.4 copy.42
  241.7 0.7 fusion.5
  242.4 0.7 reshape.211
  243.1 4.5 %divide_subtract_fusion = (f32[2,64,4,512]{3,2,1,0:T(4,128)S(1)}, f32[2,64,4,512]{3,2,1,0:T(4,128)}, f32[2,64,4,512]{3,2,1,0:T(4,128)}) fusion(f32[2,64,4,512]{3,2,1,0:T(4,128)} %param.10, f32[2,64,4,512]{3,2,1,0:T(4,128)S(1)} %reshape.211, f32[2,64,4,512]{3,2,1,0:T(4,128)} %param.11, f32[2,64,4,512]{3,2,1,0:T(4,128)} %param.12), kind=kLoop, calls=%fused_computation.18 | loop fusion | flops 2883584 | bytes 7340032 | tf_op jit(solution)/shard_map/sub | solution.py:90
  247.7 0.7 reshape.212
  248.4 1.2 gather_fusion
  250.2 15.6 %all_to_all.11 = f32[2,8,1,4,4,512]{5,4,3,2,0,1:T(4,128)} all-to-all(f32[2,8,1,4,4,512]{5,4,3,2,0,1:T(4,128)S(1)} %copy_select_fusion), channel_id=1, replica_groups=mesh['table'=8,'ray'=16] {'table'}, dimensions={1} | all-to-all | bytes 1048576 | tf_op jit(solution)/shard_map/all_to_all | solution.py:94
  265.8 68.7 %all-gather.2.cloned.1.call-done = f32[2,8,16,4,4,512]{5,4,3,2,0,1:T(4,128)} async-done(((f32[2,8,1,4,4,512]{5,4,3,2,0,1:T(4,128)}), f32[2,8,16,4,4,512]{5,4,3,2,0,1:T(4,128)}) %all-gather.2.cloned.1.call-update) | async-done | bytes 8388624 | tf_op jit(solution)/shard_map/all_gather | solution.py:95
  334.5 10.3 %copy.46 = f32[2,16,8,4,4,512]{5,4,3,2,1,0:T(4,128)} copy(f32[2,16,8,4,4,512]{5,4,3,1,0,2:T(4,128)} %bitcast.63) | data formatting | bytes 16777216 | tf_op jit(solution)/shard_map/transpose | solution.py:96
  344.9 10.0 %reshape.213 = f32[2,16,128,512]{3,2,1,0:T(8,128)} reshape(f32[2,16,8,4,4,512]{5,4,3,2,1,0:T(4,128)} %copy.46) | data formatting | bytes 16777216 | tf_op jit(solution)/shard_map/reshape | solution.py:96
  354.9 12.6 %fusion.3 = f32[2,16,32,128]{3,2,1,0:T(8,128)S(1)} fusion(f32[2,16,128,512]{3,2,1,0:T(8,128)} %reshape.213, f32[2,16,32]{2,1,0:T(8,128)S(1)} %broadcast_in_dim.107, s32[2,16,32]{2,1,0:T(8,128)S(1)} %get-tuple-element.8, f32[2,16,32]{2,1,0:T(8,128)S(1)} %broadcast_in_dim.105, s32[2,16,32]{2,1,0:T(8,128)S(1)} %get-tuple-element.9, ...), kind=kOutput, calls=%fused_computation.21 | convolution fusion | flops 817364992 | bytes 8978432 | tf_op jit(solution)/shard_map/lrje,lrce->lrjc/dot_general | solution.py:99
  367.6 0.9 copy.47
  369.3 0.8 convolution_bitcast_fusion
  (41 shorter events, 3.6 us)
Async XLA Ops:
  7.2 147.1 %copy-start = (s32[8,2,128,4]{2,3,1,0:T(4,128)S(1)}, s32[8,2,128,4]{2,3,1,0:T(4,128)}, u32[]{:S(2)}) copy-start(s32[8,2,128,4]{2,3,1,0:T(4,128)} %param.13) | copy-start | bytes 98308
  7.2 232.8 %reduce-scatter.4.cloned.1.call-start = ((), (), s32[]{:S(2)}) async-start(), calls=%async_computation.4 | async-start | bytes 8912896
  154.0 180.6 %all-gather.2.cloned.1.call-start = ((), (), s32[]{:S(2)}) async-start(), calls=%async_computation.3 | async-start | bytes 8912896 | tf_op jit(solution)/shard_map/all_gather | solution.py:95
  247.7 1.9 copy-start.2
  367.6 1.4 copy-start.4
  367.6 2.5 copy-start.1
  368.5 0.7 copy-start.3
Sparse Core Ops, SparseCore 0:
  154.1 85.8 reduce-scatter.3
  265.9 68.5 all-gather.1
where the time goes:
time: 378 us; the launch traced here: 377 us
  waiting for transfers between devices  154 us (41%)
  blocking collectives  115 us (30%)
  local copies, waits for them, and re-layouts  60.9 us (16%)
  matrix products  25.7 us (7%)
  between operations  14.3 us (4%)
  other arithmetic  6.83 us (2%)
    all_to_all x1, blocking collectives, on_device(): lax.all_to_all(partial_value, 'table', split_axis=1, concat_axis=1, tiled...  99.5 us
    unnamed x3, waiting for transfers between devices  85.1 us
    all_gather x1, waiting for transfers between devices, on_device(): fetched = lax.all_gather(returned, 'ray', axis=2, tiled=True)  68.7 us
    reshape x2, local copies, waits for them, and re-layouts, on_device(): partial_value.reshape(levels, ray_size, table_size, slot_count, 4, block_...  20.1 us
    all_to_all x1, blocking collectives, on_device(): lax.all_to_all(picked, 'table', split_axis=1, concat_axis=1, tiled=True)  15.6 us
    dot_general x1, matrix products, on_device(): jnp.einsum('lrje,lrce->lrjc', spread, run_tables, precision=lax.Precision...  12.6 us
    dot_general x1, matrix products, block_partials(): jnp.einsum('lrjc,lrje->lrce', scaled, spread, precision=lax.Precision.HIG...  11.2 us
    all_to_all x1, local copies, waits for them, and re-layouts, on_device(): lax.all_to_all(partial_value, 'table', split_axis=1, concat_axis=1, tiled...  10.9 us
  transfers between devices with their start and end apart: 2, of which 2 were waited for; matrix products, arithmetic and copies ran while one was open for 0% of the time, Pallas kernels for 0%

commit v1 on v0

--- a/solution.py
+++ b/solution.py
@@ -1,3 +1,4 @@
+import functools
 import jax
 import jax.numpy as jnp
 from jax import lax
@@ -7,6 +8,16 @@
 beta_two = 0.99
 learn_rate = 0.01
 adam_eps = 1e-15
+
+
+def _time_positions(a0, comm_axis):
+    next_value = jax.lax.all_to_all(
+        jnp.stack([a0] * jax.lax.axis_size(comm_axis), axis=0), comm_axis, 0, 0
+    )
+    return jnp.concatenate(next_value, 2)
+
+
+view_rings = functools.partial(_time_positions, comm_axis="ray")
 
 
 def hat_weights(fractions):
@@ -92,7 +103,7 @@
     picked = jnp.take_along_axis(flat_table, requests[:, :, None], axis=1)
     picked = picked.reshape(levels, table_size, 1, slot_count, 4, block_rows)
     returned = lax.all_to_all(picked, "table", split_axis=1, concat_axis=1, tiled=True)
-    fetched = lax.all_gather(returned, "ray", axis=2, tiled=True)
+    fetched = view_rings(returned)
     run_tables = jnp.transpose(fetched, (0, 2, 1, 3, 4, 5)).reshape(
         levels, ray_size, candidates * 4, block_rows
     )

time: 378 us -> 401 us (1.061)
  blocking collectives: 115 us -> 214 us
  waiting for transfers between devices: 154 us -> 85.3 us
  local copies, waits for them, and re-layouts: 60.9 us -> 52.9 us
    all_to_all x0 -> x1, blocking collectives: none -> 98.7 us  [_time_positions(): jax.lax.all_to_all(jnp.stack([a0] * jax.lax.axis_size(comm_axis), axis=0)...]
    all_gather x1 -> x0, waiting for transfers between devices: 68.7 us -> none  [on_device(): fetched = lax.all_gather(returned, 'ray', axis=2, tiled=True)]
    transpose x1 -> x0, local copies, waits for them, and re-layouts: 10.3 us -> none  [on_device(): jnp.transpose(fetched, (0, 2, 1, 3, 4, 5))]
    unnamed x3 -> x2, waiting for transfers between devices: 85.1 us -> 85.3 us
  transfers between devices with their start and end apart: 2 -> 1, of which waited for: 2 -> 1; matrix products, arithmetic and copies ran while one was open for 0% -> 0% of each run, Pallas kernels for 0% -> 0%
where the time goes in v1:
time: 401 us; the launch traced here: 399 us
  blocking collectives  214 us (53%)
  waiting for transfers between devices  85.3 us (21%)
  local copies, waits for them, and re-layouts  52.9 us (13%)
  matrix products  25.6 us (6%)
  between operations  14.3 us (4%)
  other arithmetic  6.83 us (2%)
    all_to_all x1, blocking collectives, on_device(): lax.all_to_all(partial_value, 'table', split_axis=1, concat_axis=1, tiled...  99.5 us
    all_to_all x1, blocking collectives, _time_positions(): jax.lax.all_to_all(jnp.stack([a0] * jax.lax.axis_size(comm_axis), axis=0)...  98.7 us
    unnamed x2, waiting for transfers between devices  85.3 us
    reshape x2, local copies, waits for them, and re-layouts, on_device(): partial_value.reshape(levels, ray_size, table_size, slot_count, 4, block_...  20.1 us
    all_to_all x1, blocking collectives, on_device(): lax.all_to_all(picked, 'table', split_axis=1, concat_axis=1, tiled=True)  15.5 us
    dot_general x1, matrix products, on_device(): jnp.einsum('lrje,lrce->lrjc', spread, run_tables, precision=lax.Precision...  12.6 us
    dot_general x1, matrix products, block_partials(): jnp.einsum('lrjc,lrje->lrce', scaled, spread, precision=lax.Precision.HIG...  11.2 us
    all_to_all x1, local copies, waits for them, and re-layouts, on_device(): lax.all_to_all(partial_value, 'table', split_axis=1, concat_axis=1, tiled...  10.9 us
  transfers between devices with their start and end apart: 1, of which 1 were waited for; matrix products, arithmetic and copies ran while one was open for 0% of the time, Pallas kernels for 0%

profile of v1, /device:TPU:1, one launch (start us, length us, event | category | flops | bytes accessed | tf_op | source)
XLA Modules:
  0.0 398.8 jit_solution(11958786808203050054)
XLA Ops:
  7.2 0.7 fusion.15
  8.0 0.7 fusion.17
  8.8 0.8 reshape.215
  10.1 0.8 reshape.216
  10.9 0.8 reshape.217
  12.1 11.2 %fusion.2 = f32[2,16,128,512]{3,2,1,0:T(8,128)} fusion(f32[2,16,32,128]{2,1,3,0:T(8,128)S(1)} %bitcast.70, f32[2,16,32]{2,1,0:T(8,128)S(1)} %broadcast_in_dim.107, s32[2,16,32]{2,1,0:T(8,128)S(1)} %get-tuple-element.8, f32[2,16,32]{2,1,0:T(8,128)S(1)} %broadcast_in_dim.105, s32[2,16,32]{2,1,0:T(8,128)S(1)} %get-tuple-element.9, ...), kind=kOutput, calls=%fused_computation.4 | convolution fusion | flops 817364992 | bytes 8978432 | tf_op jit(solution)/shard_map/lrjc,lrje->lrce/dot_general | solution.py:55
  23.4 9.8 %reshape.218 = f32[2,16,8,4,4,512]{5,4,3,2,1,0:T(4,128)} reshape(f32[2,16,128,512]{3,2,1,0:T(8,128)} %fusion.2) | data formatting | bytes 16777216 | tf_op jit(solution)/shard_map/reshape | solution.py:88
  33.2 10.3 %copy.55 = f32[2,16,8,4,4,512]{5,4,3,1,0,2:T(4,128)} copy(f32[2,16,8,4,4,512]{5,4,3,2,1,0:T(4,128)} %reshape.218) | data formatting | bytes 16777216 | tf_op jit(solution)/shard_map/reshape | solution.py:88
  43.5 99.5 %all_to_all.18 = f32[2,8,16,4,4,512]{5,4,3,2,0,1:T(4,128)S(1)} all-to-all(f32[2,8,16,4,4,512]{5,4,3,2,0,1:T(4,128)} %bitcast.67), channel_id=1, replica_groups=mesh['table'=8,'ray'=16] {'table'}, dimensions={1} | all-to-all | bytes 16777216 | tf_op jit(solution)/shard_map/all_to_all | solution.py:90
  143.0 10.9 %copy.40 = f32[2,8,16,4,4,512]{5,1,4,3,0,2:T(8,128)} copy(f32[2,8,16,4,4,512]{5,4,3,2,0,1:T(4,128)S(1)} %all_to_all.18) | data formatting | bytes 16777216 | tf_op jit(solution)/shard_map/all_to_all | solution.py:90
  154.7 85.3 %reduce-scatter.4.cloned.1.call-done = f32[2,8,1,4,4,512]{5,1,4,3,0,2:T(8,128)} async-done(((f32[2,8,16,4,4,512]{5,1,4,3,0,2:T(8,128)}), f32[2,8,1,4,4,512]{5,1,4,3,0,2:T(8,128)}) %reduce-scatter.4.cloned.1.call-update) | async-done | bytes 524304
  240.0 1.4 copy.41
  241.7 0.7 fusion.6
  242.4 0.7 reshape.220
  243.1 4.5 %divide_subtract_fusion = (f32[2,64,4,512]{3,2,1,0:T(4,128)S(1)}, f32[2,64,4,512]{3,2,1,0:T(4,128)}, f32[2,64,4,512]{3,2,1,0:T(4,128)}) fusion(f32[2,64,4,512]{3,2,1,0:T(4,128)} %param.10, f32[2,64,4,512]{3,2,1,0:T(4,128)S(1)} %reshape.220, f32[2,64,4,512]{3,2,1,0:T(4,128)} %param.11, f32[2,64,4,512]{3,2,1,0:T(4,128)} %param.12), kind=kLoop, calls=%fused_computation.20 | loop fusion | flops 2883584 | bytes 7340032 | tf_op jit(solution)/shard_map/sub | solution.py:101
  247.7 0.9 reshape.221
  248.6 1.2 gather_fusion
  250.4 15.5 %all_to_all.19 = f32[2,8,1,4,4,512]{5,4,3,0,2,1:T(4,128)S(1)} all-to-all(f32[2,8,1,4,4,512]{5,4,3,0,2,1:T(4,128)S(1)} %copy_select_fusion), channel_id=1, replica_groups=mesh['table'=8,'ray'=16] {'table'}, dimensions={1} | all-to-all | bytes 1048576 | tf_op jit(solution)/shard_map/all_to_all | solution.py:105
  266.0 2.1 stack.2
  268.1 98.7 %all_to_all.20 = f32[16,2,8,1,4,4,512]{6,5,4,2,1,3,0:T(4,128)} all-to-all(f32[16,2,8,1,4,4,512]{6,5,4,2,1,3,0:T(4,128)S(1)} %stack.2), channel_id=1, replica_groups=mesh['table'=8,'ray'=16] {'ray'}, dimensions={0} | all-to-all | bytes 16777216 | tf_op jit(solution)/shard_map/all_to_all | solution.py:14
  366.8 10.0 %reshape.234 = f32[2,16,128,512]{3,2,0,1:T(8,128)} reshape(f32[2,16,8,4,4,512]{5,4,3,2,0,1:T(4,128)} %bitcast.68) | data formatting | bytes 16777216 | tf_op jit(solution)/shard_map/reshape | solution.py:107
  376.8 12.6 %fusion = f32[2,16,32,128]{3,2,1,0:T(8,128)S(1)} fusion(f32[2,16,128,512]{3,2,0,1:T(8,128)} %reshape.234, f32[2,16,32]{2,1,0:T(8,128)S(1)} %broadcast_in_dim.107, s32[2,16,32]{2,1,0:T(8,128)S(1)} %get-tuple-element.8, f32[2,16,32]{2,1,0:T(8,128)S(1)} %broadcast_in_dim.105, s32[2,16,32]{2,1,0:T(8,128)S(1)} %get-tuple-element.9, ...), kind=kOutput, calls=%fused_computation.1 | convolution fusion | flops 817364992 | bytes 8978432 | tf_op jit(solution)/shard_map/lrje,lrce->lrjc/dot_general | solution.py:110
  389.5 0.9 copy.47
  391.1 0.8 convolution_bitcast_fusion
  (40 shorter events, 3.4 us)
Async XLA Ops:
  7.2 146.8 %copy-start = (s32[8,2,128,4]{2,3,1,0:T(4,128)S(1)}, s32[8,2,128,4]{2,3,1,0:T(4,128)}, u32[]{:S(2)}) copy-start(s32[8,2,128,4]{2,3,1,0:T(4,128)} %param.13) | copy-start | bytes 98308
  7.2 232.8 %reduce-scatter.4.cloned.1.call-start = ((), (), s32[]{:S(2)}) async-start(), calls=%async_computation.4 | async-start | bytes 8912896
  247.7 2.2 copy-start.2
  389.4 1.4 copy-start.4
  389.5 2.5 copy-start.1
  390.4 0.7 copy-start.3
Sparse Core Ops, SparseCore 0:
  154.1 85.8 reduce-scatter.3
